TPU v7x, 256 devices: a whole 4x4x8 slice. The times are simulated.
256 devices in a mesh: frames: 16 (over z, core), mp: 16 (over y, x).
Axes of the slice: x: 4, y: 4, z: 8, core: 2. Of those that a mesh axis runs over, the one named last changes fastest.
Arguments:
- motion: bfloat16 [256, 25, 1024], P('frames', None, 'mp'), may hold values from -6 to 6
- adjacency: float32 [2, 25, 25], replicated, may hold values from -1.25 to 1.25
- w_bc: bfloat16 [2, 1024, 128], P(None, 'mp'), may hold values from -0.1875 to 0.1875
- decay: float32 [2, 256, 1024], P(None, 'frames', 'mp'), may hold values from 0.5 to 1, as said below
- skip: float32 [2, 1024], P(None, 'mp'), may hold values from 0.5 to 1.5
- w_out: bfloat16 [2, 1024, 1024], P(None, 'mp'), may hold values from -0.25 to 0.25
Outputs:
- encoded: float32 [256, 25, 1024], P('frames', None, 'mp')
Inputs may be any that keep to these rules, and one draw needn't show every extreme that they name: `decay`: each entry lies strictly between 0 and 1.
All inputs are finite; a program needn't handle non-finite values.
Results may differ from a plain program's by a relative error of at most 0.012.
Values may be sent and summed in bfloat16 or wider, within the bound.
A program may use at most 64 MiB of HBM per device.

v0:
```python
import jax
import jax.numpy as jnp
from jax import lax
from jax.sharding import PartitionSpec as P

ENCODER_LAYERS = 2


def entering(value, axis, join, neutral):
    count, mine = (lax.axis_size(axis), lax.axis_index(axis))
    pieces = jax.tree.map(lambda part: lax.all_gather(part, axis), value)
    so_far = jax.tree.map(
        lambda part, zero: jnp.full_like(part, 0) + jnp.asarray(zero, part.dtype), value, neutral
    )

    def lap(position, so_far):
        longer = join(so_far, jax.tree.map(lambda part: part[position], pieces))
        return jax.tree.map(lambda new, old: jnp.where(position < mine, new, old), longer, so_far)

    return lax.fori_loop(0, count - 1, lap, so_far)


def shards(motion, adjacency, w_bc, decay, skip, w_out):
    highest = lax.Precision.HIGHEST
    frames_loc, joints, width_loc = motion.shape
    state = w_bc.shape[2] // 2
    x = motion.astype(jnp.float32)
    for layer in range(ENCODER_LAYERS):
        mixed = jnp.einsum("jk,tkd->tjd", adjacency[layer], x, precision=highest).astype(
            jnp.bfloat16
        )
        partial_coef = jnp.dot(
            mixed.reshape(-1, width_loc), w_bc[layer], preferred_element_type=jnp.float32
        )
        coef = lax.psum(partial_coef, "mp").reshape(frames_loc, joints, 2 * state)
        in_b = coef[:, :, :state]
        out_c = coef[:, :, state:]
        decay_speed = decay[layer]
        logs = jnp.cumsum(jnp.log(decay_speed), axis=0)
        upto = jnp.exp(logs)
        weighted = (
            (1.0 - decay_speed)[:, None, :] * mixed.astype(jnp.float32) * jnp.exp(-logs)[:, None, :]
        )
        later = lax.broadcasted_iota(jnp.int32, (frames_loc, frames_loc), 0)
        earlier = lax.broadcasted_iota(jnp.int32, (frames_loc, frames_loc), 1)
        grid = jnp.einsum("tjn,sjn->jts", out_c, in_b, precision=highest)
        grid = jnp.where((earlier <= later)[None], grid, 0.0)
        inner = upto[:, None, :] * jnp.einsum("jts,sjd->tjd", grid, weighted, precision=highest)
        total = upto[-1]
        end_state = jnp.einsum(
            "sjd,sjn->jdn", weighted * total[None, None, :], in_b, precision=highest
        )

        def link(first, second):
            return (first[0] * second[0], second[0][None, :, None] * first[1] + second[1])

        _, incoming = entering(
            (total, end_state), "frames", link, (jnp.ones_like(total), jnp.zeros_like(end_state))
        )
        outer = upto[:, None, :] * jnp.einsum("tjn,jdn->tjd", out_c, incoming, precision=highest)
        result = (inner + outer + skip[layer][None, None, :] * mixed.astype(jnp.float32)).astype(
            jnp.bfloat16
        )
        flat = result.reshape(-1, width_loc)
        weights = w_out[layer]
        summed = lax.psum_scatter(
            lax.dot_general(
                weights, flat, (((0,), (1,)), ((), ())), preferred_element_type=jnp.float32
            ),
            "mp",
            scatter_dimension=0,
            tiled=True,
        )
        update = summed.T.reshape(frames_loc, joints, width_loc)
        x = x + update
    return x


def solution(mesh):
    return jax.shard_map(
        shards,
        mesh=mesh,
        in_specs=(
            P("frames", None, "mp"),
            P(),
            P(None, "mp", None),
            P(None, "frames", "mp"),
            P(None, "mp"),
            P(None, "mp", None),
        ),
        out_specs=P("frames", None, "mp"),
        check_vma=False,
    )
```

profile of v0, /device:TPU:1, one launch (start us, length us, event | category | flops | bytes accessed | tf_op | source)
XLA Modules:
  0.0 580.0 jit_solution(17792508891115939289)
XLA Ops:
  7.4 1.1 fusion.36
  10.6 96.2 %all-reduce.3.cloned.1.call-done = f32[16,25,128]{2,0,1:T(8,128)} async-done(((f32[16,25,128]{2,0,1:T(8,128)}), f32[16,25,128]{2,0,1:T(8,128)}) %all-reduce.3.cloned.1.call-update) | async-done | bytes 204816 | tf_op jit(solution)/shard_map/psum | solution.py:35
  106.8 3.4 fusion.13
  110.3 19.7 %all-gather.2 = f32[16,1,64]{2,1,0:T(1,128)S(1)} all-gather(f32[1,1,64]{2,1,0:T(1,128)S(1)} %get-tuple-element.264), channel_id=1, replica_groups=mesh['frames'=16,'mp'=16] {'frames'}, dimensions={0}, use_global_device_ids=true | all-gather | bytes 4352 | tf_op jit(solution)/shard_map/all_gather | solution.py:11
  130.5 59.1 %all-gather.7.cloned.1.call-done = f32[400,64,64]{2,1,0:T(8,128)} async-done(((f32[25,64,64]{2,1,0:T(8,128)}), f32[400,64,64]{2,1,0:T(8,128)}) %all-gather.7.cloned.1.call-update) | async-done | bytes 6553616 | tf_op jit(solution)/shard_map/all_gather | solution.py:11
  189.7 21.0 %while.28 = (s32[]{:T(128)}, f32[25,64,64]{2,1,0:T(8,128)S(1)}, s32[]{:T(128)}, f32[16,64]{1,0:T(8,128)S(1)}, f32[16,25,64,64]{3,2,1,0:T(8,128)}, /*index=5*/s32[]{:T(128)}, s32[]{:T(128)}) while((s32[]{:T(128)}, f32[25,64,64]{2,1,0:T(8,128)S(1)}, s32[]{:T(128)}, f32[16,64]{1,0:T(8,128)S(1)}, f32[16,25,64,64]{3,2,1,0:T(8,128)}, ...), condition=%wide.region_3.4_spmd.clone, body=%wide.region_2.3_spmd.clone.sunk | while | flops 409604 | bytes 1229673 | solution.py:20
  189.7 1.4 fusion.68
  191.1 1.4 fusion.68
  192.5 1.4 fusion.68
  193.9 1.4 fusion.68
  195.3 1.4 fusion.68
  196.7 1.4 fusion.68
  198.1 1.4 fusion.68
  199.5 1.4 fusion.68
  200.9 1.4 fusion.68
  202.3 1.4 fusion.68
  203.7 1.4 fusion.68
  205.1 1.4 fusion.68
  206.5 1.4 fusion.68
  207.9 1.4 fusion.68
  209.3 1.4 fusion.68
  210.7 1.4 fusion.27
  213.0 1.8 copy.66
  214.9 75.9 %reduce-scatter.7.cloned.1.call-done = f32[64,400]{1,0:T(8,128)} async-done(((f32[1024,400]{1,0:T(8,128)}), f32[64,400]{1,0:T(8,128)}) %reduce-scatter.7.cloned.1.call-update) | async-done | bytes 102416
  290.8 1.0 copy.67
  293.5 93.7 %all-reduce.5.cloned.1.call-done = f32[16,25,128]{2,0,1:T(8,128)} async-done(((f32[16,25,128]{2,0,1:T(8,128)}), f32[16,25,128]{2,0,1:T(8,128)}) %all-reduce.5.cloned.1.call-update) | async-done | bytes 204816 | tf_op jit(solution)/shard_map/psum | solution.py:35
  387.2 3.4 fusion.18
  390.7 19.7 %all-gather.3 = f32[16,1,64]{2,1,0:T(1,128)S(1)} all-gather(f32[1,1,64]{2,1,0:T(1,128)S(1)} %get-tuple-element.260), channel_id=1, replica_groups=mesh['frames'=16,'mp'=16] {'frames'}, dimensions={0}, use_global_device_ids=true | all-gather | bytes 4352 | tf_op jit(solution)/shard_map/all_gather | solution.py:11
  410.9 59.2 %all-gather.9.cloned.1.call-done = f32[400,64,64]{2,1,0:T(8,128)} async-done(((f32[25,64,64]{2,1,0:T(8,128)}), f32[400,64,64]{2,1,0:T(8,128)}) %all-gather.9.cloned.1.call-update) | async-done | bytes 6553616 | tf_op jit(solution)/shard_map/all_gather | solution.py:11
  470.1 21.0 %while.29 = (s32[]{:T(128)}, f32[25,64,64]{2,1,0:T(8,128)S(1)}, s32[]{:T(128)}, f32[16,64]{1,0:T(8,128)S(1)}, f32[16,25,64,64]{3,2,1,0:T(8,128)}, /*index=5*/s32[]{:T(128)}, s32[]{:T(128)}) while((s32[]{:T(128)}, f32[25,64,64]{2,1,0:T(8,128)S(1)}, s32[]{:T(128)}, f32[16,64]{1,0:T(8,128)S(1)}, f32[16,25,64,64]{3,2,1,0:T(8,128)}, ...), condition=%wide.region_8.9_spmd.clone, body=%wide.region_7.8_spmd.clone.sunk | while | flops 409604 | bytes 1229673 | solution.py:20
  470.1 1.4 fusion.69
  471.5 1.4 fusion.69
  472.9 1.4 fusion.69
  474.3 1.4 fusion.69
  475.7 1.4 fusion.69
  477.1 1.4 fusion.69
  478.5 1.4 fusion.69
  479.9 1.4 fusion.69
  481.3 1.4 fusion.69
  482.7 1.4 fusion.69
  484.1 1.4 fusion.69
  485.5 1.4 fusion.69
  486.9 1.4 fusion.69
  488.3 1.4 fusion.69
  489.7 1.4 fusion.69
  491.1 1.4 fusion.22
  493.4 1.8 copy.68
  495.2 76.0 %reduce-scatter.9.cloned.1.call-done = f32[64,400]{1,0:T(8,128)} async-done(((f32[1024,400]{1,0:T(8,128)}), f32[64,400]{1,0:T(8,128)}) %reduce-scatter.9.cloned.1.call-update) | async-done | bytes 102416
  (96 shorter events, 9.5 us)
Async XLA Ops:
  6.5 4.0 copy-start.5
  6.5 100.3 %all-reduce.3.cloned.1.call-start = ((), (), s32[]{:S(2)}) async-start(), calls=%async_computation.2 | async-start | bytes 409600 | tf_op jit(solution)/shard_map/psum | solution.py:35
  8.5 121.5 %copy-start.6 = (f32[2,64]{1,0:T(2,128)S(1)}, f32[2,64]{1,0:T(2,128)}, u32[]{:S(2)}) copy-start(f32[2,64]{1,0:T(2,128)} %param.14) | copy-start | bytes 1540
  10.5 179.2 %all-gather.7.cloned.1.call-start = ((), (), s32[]{:S(2)}) async-start(), calls=%async_computation.4 | async-start | bytes 13926400 | tf_op jit(solution)/shard_map/all_gather | solution.py:11
  106.8 23.2 %copy-start = (f32[16,25,128]{2,0,1:T(8,128)S(1)}, f32[16,25,128]{2,0,1:T(8,128)}, u32[]{:S(2)}) copy-start(f32[16,25,128]{2,0,1:T(8,128)} %all-reduce.3.cloned.1.call-done) | copy-start | bytes 614404
  110.2 180.6 %reduce-scatter.7.cloned.1.call-start = ((), (), s32[]{:S(2)}) async-start(), calls=%async_computation.6 | async-start | bytes 2228224
  210.7 1.9 copy-start.3
  214.8 77.1 %copy-start.2 = (bf16[16,25,64]{2,0,1:T(8,128)(2,1)S(1)}, bf16[16,25,64]{2,0,1:T(8,128)(2,1)}, u32[]{:S(2)}) copy-start(bf16[16,25,64]{2,0,1:T(8,128)(2,1)} %param.10) | copy-start | bytes 153604
  214.8 77.6 %copy-start.4 = (bf16[2,64,128]{2,1,0:T(8,128)(2,1)S(1)}, bf16[2,64,128]{2,1,0:T(8,128)(2,1)}, u32[]{:S(2)}) copy-start(bf16[2,64,128]{2,1,0:T(8,128)(2,1)} %param.12) | copy-start | bytes 98308
  214.8 172.4 %all-reduce.5.cloned.1.call-start = ((), (), s32[]{:S(2)}) async-start(), calls=%async_computation.3 | async-start | bytes 409600 | tf_op jit(solution)/shard_map/psum | solution.py:35
  293.4 176.7 %all-gather.9.cloned.1.call-start = ((), (), s32[]{:S(2)}) async-start(), calls=%async_computation.5 | async-start | bytes 13926400 | tf_op jit(solution)/shard_map/all_gather | solution.py:11
  387.2 23.2 %copy-start.1 = (f32[16,25,128]{2,0,1:T(8,128)S(1)}, f32[16,25,128]{2,0,1:T(8,128)}, u32[]{:S(2)}) copy-start(f32[16,25,128]{2,0,1:T(8,128)} %all-reduce.5.cloned.1.call-done) | copy-start | bytes 614404
  390.6 180.6 %reduce-scatter.9.cloned.1.call-start = ((), (), s32[]{:S(2)}) async-start(), calls=%async_computation.7 | async-start | bytes 2228224
Sparse Core Ops, SparseCore 0:
  10.6 96.2 all-reduce.2
  110.3 79.2 all-gather.6
  214.9 75.8 reduce-scatter.6
  293.8 93.3 all-reduce.4
  390.8 79.2 all-gather.8
  495.3 75.8 reduce-scatter.8
where the time goes:
time: 582 us; the launch traced here: 580 us
  waiting for transfers between devices  460 us (79%)
  other arithmetic  40.9 us (7%)
  blocking collectives  39.4 us (7%)
  matrix products  14.6 us (3%)
  between operations  13.8 us (2%)
  local copies, waits for them, and re-layouts  9.76 us (2%)
    psum x2, waiting for transfers between devices, shards(): coef = lax.psum(partial_coef, 'mp').reshape(frames_loc, joints, 2 * state)  190 us
    unnamed x8, waiting for transfers between devices  152 us
    all_gather x2, waiting for transfers between devices, entering(): pieces = jax.tree.map(lambda part: lax.all_gather(part, axis), value)  118 us
    select_n x30, other arithmetic, lap(): jnp.where(position < mine, new, old)  40.7 us
    all_gather x2, blocking collectives, entering(): pieces = jax.tree.map(lambda part: lax.all_gather(part, axis), value)  39.4 us
  transfers between devices with their start and end apart: 6, of which 6 were waited for; matrix products, arithmetic and copies ran while one was open for 0% of the time, Pallas kernels for 0%

commit v1 on v0

v1 whole, which is shorter than its diff:
```python
import functools

import jax
import jax.numpy as jnp
from jax import lax
from jax.experimental import pallas as pl
from jax.experimental.pallas import tpu as pltpu
from jax.sharding import PartitionSpec as P

MESH = pl.DeviceIdType.MESH
HI = lax.Precision.HIGHEST
F32, BF16 = jnp.float32, jnp.bfloat16
LAYERS = 2
G = 16
HALF, PAIR = 64, 128
FRAMES = 256
CHUNK = 128


def left_half(shape):
    return lax.broadcasted_iota(jnp.int32, shape, len(shape) - 1) % PAIR < HALF


def mix_halves(first, second):
    left = left_half(first.shape)
    return (
        jnp.where(left, first, pltpu.roll(second, HALF, 1)),
        jnp.where(left, pltpu.roll(first, HALF, 1), second),
    )


def body(
    x_ref, a_ref, wbc_ref, dec_ref, skip_ref, wout_ref, out_ref,
    xbuf, wbc, wout, dsend, dall, scale_e, scale_w, scale_x, scale_f,
    send_a, buf_a, send_b, buf_b, send_c, buf_c, send_d, buf_d, send_e, buf_e,
    tmp, xs, res, ssem, rsem,
):
    b, c = lax.axis_index("frames"), lax.axis_index("mp")

    def at(axis, peer):
        return (b, peer) if axis == "mp" else (peer, c)

    def peers(axis, act):
        me = c if axis == "mp" else b

        def one(k, carry):
            act(lax.rem(me + k, G))
            return carry

        lax.fori_loop(1, G, one, 0)

    def send(axis, n, src, dst):
        me = c if axis == "mp" else b
        peers(
            axis,
            lambda peer: pltpu.make_async_remote_copy(
                src_ref=src(peer),
                dst_ref=dst.at[me],
                send_sem=ssem.at[n],
                recv_sem=rsem.at[n],
                device_id=at(axis, peer),
                device_id_type=MESH,
            ).start(),
        )

    def wait(sem, n, dst):
        all_but_mine = dst.at[pl.ds(0, G - 1)]
        pltpu.make_async_copy(all_but_mine, all_but_mine, sem.at[n]).wait()

    barrier = pltpu.get_barrier_semaphore()
    for axis in ("mp", "frames"):
        peers(
            axis,
            lambda peer, axis=axis: pl.semaphore_signal(
                barrier, inc=1, device_id=at(axis, peer), device_id_type=MESH
            ),
        )
    dsend[...] = jnp.concatenate([dec_ref[0], dec_ref[1]], axis=1)
    pl.semaphore_wait(barrier, 2 * (G - 1))

    NX, ND, NBC, NOUT, NE, NL = 0, 1, 2, 4, 6, 7
    send("mp", NX, lambda peer: x_ref.at[peer], xbuf)
    send("mp", NBC, lambda peer: wbc_ref.at[0], wbc.at[0])
    send("frames", ND, lambda peer: dsend, dall)
    send("mp", NBC + 1, lambda peer: wbc_ref.at[1], wbc.at[1])
    for layer in range(LAYERS):
        send("mp", NOUT + layer, lambda peer, layer=layer: wout_ref.at[layer], wout.at[layer])

    xbuf[c] = x_ref[c]
    dall[b] = dsend[...]
    for layer in range(LAYERS):
        wbc[layer, c] = wbc_ref[layer]
        wout[layer, c] = wout_ref[layer]

    def spread(buf, dst, add):
        for q in range(G // 2):
            even, odd = mix_halves(buf[2 * q].astype(F32), buf[2 * q + 1].astype(F32))
            lanes = pl.ds(q * PAIR, PAIR)
            dst[pl.ds(0, G), lanes] = even.astype(dst.dtype)
            dst[pl.ds(G, G), lanes] = odd.astype(dst.dtype)

    wait(rsem, NX, xbuf)
    spread(xbuf, xs, False)

    for layer in range(LAYERS):
        base = NL + 4 * layer
        mixed = jnp.dot(a_ref[layer], xs[...], precision=HI, preferred_element_type=F32).astype(BF16)
        if layer == 0:
            wait(rsem, NBC, wbc.at[0])
        else:
            wait(rsem, NBC + 1, wbc.at[1])
        coef = jnp.dot(
            mixed, wbc[layer].reshape(G * HALF, PAIR), preferred_element_type=F32
        )
        in_b, out_c = mix_halves(coef[:G], coef[G:])
        mixed32 = mixed.astype(F32)
        for q in range(G // 2):
            lanes = slice(q * PAIR, (q + 1) * PAIR)
            pieces = mix_halves(mixed32[:G, lanes], mixed32[G:, lanes])
            for i in range(2):
                send_a[layer, 2 * q + i, :, pl.ds(0, PAIR)] = pieces[i].astype(BF16)
                send_a[layer, 2 * q + i, :, pl.ds(PAIR, PAIR)] = in_b.astype(BF16)
                send_a[layer, 2 * q + i, :, pl.ds(2 * PAIR, PAIR)] = out_c.astype(BF16)
        send("mp", base, lambda peer: send_a.at[layer, peer], buf_a.at[layer])
        buf_a[layer, c] = send_a[layer, c]

        if layer == 0:
            wait(rsem, ND, dall)
            a = dall[...].reshape(FRAMES, PAIR)
            later = lax.broadcasted_iota(jnp.int32, (FRAMES, FRAMES), 0)
            earlier = lax.broadcasted_iota(jnp.int32, (FRAMES, FRAMES), 1)
            logs = jnp.dot(
                (earlier <= later).astype(F32), jnp.log(a), precision=HI, preferred_element_type=F32
            )
            for l in range(LAYERS):
                lanes = left_half((FRAMES, PAIR))
                mine = lanes if l == 0 else jnp.logical_not(lanes)
                la = jnp.where(mine, logs, pltpu.roll(logs, HALF, 1))
                da = 1.0 - jnp.where(mine, a, pltpu.roll(a, HALF, 1))
                for t in range(FRAMES // CHUNK):
                    rows = slice(t * CHUNK, (t + 1) * CHUNK)
                    rel = la[rows] - la[t * CHUNK + CHUNK // 2 - 1 : t * CHUNK + CHUNK // 2]
                    scale_e[l, pl.ds(t * CHUNK, CHUNK)] = jnp.exp(rel)
                    scale_w[l, pl.ds(t * CHUNK, CHUNK)] = da[rows] * jnp.exp(-rel)
                end = la[CHUNK - 1 : CHUNK]
                scale_x[l] = da[:CHUNK] * jnp.exp(end - la[:CHUNK])
                scale_f[l] = jnp.exp(la[CHUNK:] - end)

        wait(rsem, base, buf_a.at[layer])
        for part in range(3):
            tmp[part] = buf_a[layer, :, :, pl.ds(part * PAIR, PAIR)].reshape(FRAMES, PAIR).astype(F32)
        for pair in range(G):
            for part in range(3):
                send_b[layer, pair, :, pl.ds(part * PAIR, PAIR)] = tmp[
                    part, pl.ds(pair, G, stride=G), :
                ].astype(BF16)
        send("frames", base + 1, lambda peer: send_b.at[layer, peer], buf_b.at[layer])
        buf_b[layer, b] = send_b[layer, b]

        wait(rsem, base + 1, buf_b.at[layer])
        rows = buf_b[layer].reshape(FRAMES, 3 * PAIR)
        m, bp, cp = rows[:, :PAIR].astype(F32), rows[:, PAIR : 2 * PAIR], rows[:, 2 * PAIR :]
        v = (m * scale_w[layer]).astype(BF16)
        vx = (m[:CHUNK] * scale_x[layer]).astype(BF16)
        left = left_half((FRAMES, PAIR))
        c32 = cp.astype(F32)
        causal = lax.broadcasted_iota(jnp.int32, (CHUNK, CHUNK), 1) <= lax.broadcasted_iota(
            jnp.int32, (CHUNK, CHUNK), 0
        )
        over_n = (((1,), (1,)), ((), ()))

        def product(cj, bj, value, masked):
            grid = lax.dot_general(cj, bj, over_n, preferred_element_type=F32)
            if masked:
                grid = jnp.where(causal, grid, 0.0)
            return jnp.dot(grid.astype(BF16), value, preferred_element_type=F32)

        both = []
        for j in range(2):
            cj = jnp.where(left if j == 0 else jnp.logical_not(left), c32, 0.0).astype(BF16)
            y0 = product(cj[:CHUNK], bp[:CHUNK], v[:CHUNK], True)
            y1 = product(cj[CHUNK:], bp[CHUNK:], v[CHUNK:], True)
            yx = product(cj[CHUNK:], bp[:CHUNK], vx, False)
            both.append((y0, y1, yx))
        half = left[:CHUNK]
        y0, y1, yx = [jnp.where(half, p, q) for p, q in zip(*both)]
        gain = skip_ref[pl.ds(layer, 1), :]
        gain = jnp.concatenate([gain, gain], axis=1)
        low = y0 * scale_e[layer, pl.ds(0, CHUNK)] + gain * m[:CHUNK]
        high = (
            y1 * scale_e[layer, pl.ds(CHUNK, CHUNK)] + yx * scale_f[layer] + gain * m[CHUNK:]
        )
        send_c[layer, pl.ds(0, G // 2)] = low.astype(BF16).reshape(G // 2, G, PAIR)
        send_c[layer, pl.ds(G // 2, G // 2)] = high.astype(BF16).reshape(G // 2, G, PAIR)
        send("frames", base + 2, lambda peer: send_c.at[layer, peer], buf_c.at[layer])
        buf_c[layer, b] = send_c[layer, b]

        wait(rsem, base + 2, buf_c.at[layer])
        tmp[0] = buf_c[layer].reshape(FRAMES, PAIR).astype(F32)
        for frame in range(G):
            send_d[layer, frame] = tmp[0, pl.ds(frame, G, stride=G), :].astype(BF16)
        send("mp", base + 3, lambda peer: send_d.at[layer, peer], buf_d.at[layer])
        buf_d[layer, c] = send_d[layer, c]

        wait(rsem, NOUT + layer, wout.at[layer])
        wait(rsem, base + 3, buf_d.at[layer])
        spread(buf_d.at[layer], res, False)
        xs[...] += jnp.dot(
            res[...], wout[layer].reshape(G * HALF, G * HALF), preferred_element_type=F32
        )

    for q in range(G // 2):
        lanes = pl.ds(q * PAIR, PAIR)
        pieces = mix_halves(xs[pl.ds(0, G), lanes], xs[pl.ds(G, G), lanes])
        send_e[2 * q] = pieces[0]
        send_e[2 * q + 1] = pieces[1]
    send("mp", NE, lambda peer: send_e.at[peer], buf_e)
    buf_e[c] = send_e[c]
    wait(ssem, NX, xbuf)
    wait(ssem, ND, dall)
    for layer in range(LAYERS):
        base = NL + 4 * layer
        wait(ssem, NBC + layer, wbc.at[layer])
        wait(ssem, NOUT + layer, wout.at[layer])
        wait(ssem, base, buf_a.at[layer])
        wait(ssem, base + 1, buf_b.at[layer])
        wait(ssem, base + 2, buf_c.at[layer])
        wait(ssem, base + 3, buf_d.at[layer])
    wait(ssem, NE, buf_e)
    wait(rsem, NE, buf_e)
    out_ref[...] = buf_e[...]


def shards(motion, adjacency, w_bc, decay, skip, w_out):
    frames, joints, width = motion.shape
    more = 2 * G - joints
    x = jnp.pad(motion, ((0, 0), (0, more), (0, 0))).reshape(frames, G, PAIR)
    a = jnp.pad(adjacency, ((0, 0), (0, more), (0, more)))
    a = a.reshape(LAYERS, G, 2, G, 2).transpose(0, 2, 1, 4, 3).reshape(LAYERS, 2 * G, 2 * G)
    vm = pltpu.VMEM
    out = pl.pallas_call(
        body,
        out_shape=jax.ShapeDtypeStruct((G, G, PAIR), F32),
        in_specs=[pl.BlockSpec(memory_space=vm)] * 6,
        out_specs=pl.BlockSpec(memory_space=vm),
        scratch_shapes=[
            vm((G, G, PAIR), BF16),
            vm((LAYERS, G, HALF, PAIR), BF16),
            vm((LAYERS, G, HALF, G * HALF), BF16),
            vm((G, PAIR), F32),
            vm((G, G, PAIR), F32),
            vm((LAYERS, FRAMES, PAIR), F32),
            vm((LAYERS, FRAMES, PAIR), F32),
            vm((LAYERS, CHUNK, PAIR), F32),
            vm((LAYERS, CHUNK, PAIR), F32),
            vm((LAYERS, G, G, 3 * PAIR), BF16),
            vm((LAYERS, G, G, 3 * PAIR), BF16),
            vm((LAYERS, G, G, 3 * PAIR), BF16),
            vm((LAYERS, G, G, 3 * PAIR), BF16),
            vm((LAYERS, G, G, PAIR), BF16),
            vm((LAYERS, G, G, PAIR), BF16),
            vm((LAYERS, G, G, PAIR), BF16),
            vm((LAYERS, G, G, PAIR), BF16),
            vm((G, G, PAIR), F32),
            vm((G, G, PAIR), F32),
            vm((3, FRAMES, PAIR), F32),
            vm((2 * G, G * HALF), F32),
            vm((2 * G, G * HALF), BF16),
            pltpu.SemaphoreType.DMA((15,)),
            pltpu.SemaphoreType.DMA((15,)),
        ],
        compiler_params=pltpu.CompilerParams(
            collective_id=0, has_side_effects=True, vmem_limit_bytes=40 * 2**20
        ),
    )(x, a, w_bc, decay, skip, w_out)
    return out.reshape(frames, 2 * G, width)[:, :joints]


def solution(mesh):
    return jax.shard_map(
        shards,
        mesh=mesh,
        in_specs=(
            P("frames", None, "mp"),
            P(),
            P(None, "mp", None),
            P(None, "frames", "mp"),
            P(None, "mp"),
            P(None, "mp", None),
        ),
        out_specs=P("frames", None, "mp"),
        check_vma=False,
    )
```

time: 582 us -> 132 us (0.23)
  waiting for transfers between devices: 460 us -> 0 us
  Pallas kernels: 0 us -> 128 us
  other arithmetic: 40.9 us -> 0 us
  blocking collectives: 39.4 us -> 0 us
  matrix products: 14.6 us -> 0 us
  between operations: 13.8 us -> 0.09 us
  local copies, waits for them, and re-layouts: 9.76 us -> 3.78 us
    psum x2 -> x0, waiting for transfers between devices: 190 us -> none  [shards(): coef = lax.psum(partial_coef, 'mp').reshape(frames_loc, joints, 2 * state)]
    unnamed x8 -> x0, waiting for transfers between devices: 152 us -> none
    pallas_call x0 -> x1, Pallas kernels: none -> 128 us  [shards(): pl.pallas_call(body, out_shape=jax.ShapeDtypeStruct((G, G, PAIR), F32), i...]
    all_gather x2 -> x0, waiting for transfers between devices: 118 us -> none  [entering(): pieces = jax.tree.map(lambda part: lax.all_gather(part, axis), value)]
    select_n x30 -> x0, other arithmetic: 40.7 us -> none  [lap(): jnp.where(position < mine, new, old)]
    all_gather x2 -> x0, blocking collectives: 39.4 us -> none  [entering(): pieces = jax.tree.map(lambda part: lax.all_gather(part, axis), value)]
    dot_general x14 -> x0, matrix products: 14.6 us -> none  [the longest x2 6.74 us: shards(): jnp.einsum('sjd,sjn->jdn', weighted * total[None, None, :], in_b, precisi...]
  transfers between devices with their start and end apart: 6 -> 0, of which waited for: 6 -> 0; matrix products, arithmetic and copies ran while one was open for 0% -> 0% of each run, Pallas kernels for 0% -> 0%
where the time goes in v1:
time: 132 us
  Pallas kernels  128 us (97%)
  local copies, waits for them, and re-layouts  3.78 us (3%)
    pallas_call x1, Pallas kernels, shards(): pl.pallas_call(body, out_shape=jax.ShapeDtypeStruct((G, G, PAIR), F32), i...  128 us
    unnamed x13, local copies, waits for them, and re-layouts  2.68 us

profile of v1, /device:TPU:1, one launch (start us, length us, event | category | flops | bytes accessed | tf_op | source)
XLA Modules:
  0.0 131.9 jit_solution(2397177252630031790)
XLA Ops:
  0.0 0.7 copy.16
  0.8 0.3 reshape.13
  1.1 0.0 copy-start.4
  1.1 0.5 copy.12
  1.5 0.1 reshape.14.a_ref
  1.6 0.3 copy-done.4
  2.0 0.0 copy-start
  2.0 0.0 copy-start.1
  2.1 0.0 copy-start.2
  2.1 0.0 copy-start.3
  2.1 0.1 reshape.12.x_ref
  2.2 0.7 copy-done
  2.9 0.0 copy-done.1
  2.9 0.0 copy-done.2
  2.9 0.0 copy-done.3
  2.9 128.1 %shard_map.64 = f32[16,16,128]{2,1,0:T(8,128)S(1)} custom-call(bf16[16,16,128]{2,1,0:T(8,128)(2,1)S(1)} %reshape.12.x_ref, f32[2,32,32]{2,1,0:T(8,128)S(1)} %reshape.14.a_ref, bf16[2,64,128]{2,1,0:T(8,128)(2,1)S(1)} %copy-done.1, f32[2,16,64]{2,1,0:T(8,128)S(1)} %copy-done.2, f32[2,64]{1,0:T(2,128)S(1)} %copy-done.3, bf16[2,64,1024]{2,1,0:T(8,128)(2,1)S(1)} %copy-done), custom_call_target="tpu_custom_call" | custom-call | tf_op jit(solution)/shard_map/pallas_call | solution.py:241
  131.0 0.1 reshape.15
  131.1 0.8 copy.14
  (3 shorter events, 0.1 us)
Async XLA Ops:
  1.1 0.9 copy-start.4
  2.0 1.0 copy-start
  2.0 0.9 copy-start.1
  2.1 0.9 copy-start.2
  2.1 0.9 copy-start.3

commit v2 on v0

v2 whole, which is shorter than its diff:
```python
import jax
import jax.numpy as jnp
from jax import lax
from jax.experimental import pallas as pl
from jax.experimental.pallas import tpu as pltpu
from jax.sharding import PartitionSpec as P

MESH = pl.DeviceIdType.MESH
HI = lax.Precision.HIGHEST
F32, BF16 = jnp.float32, jnp.bfloat16
LAYERS = 2
JOINTS = 25
G = 16
SIDE = 4
USED = 13
HALF, PAIR = 64, 128
WIDE = G * HALF
FRAMES = 256
CHUNK = 128


def left_half(shape):
    return lax.broadcasted_iota(jnp.int32, shape, len(shape) - 1) % PAIR < HALF


def mix_halves(first, second):
    left = left_half(first.shape)
    return (
        jnp.where(left, first, pltpu.roll(second, HALF, 1)),
        jnp.where(left, pltpu.roll(first, HALF, 1), second),
    )


def body(
    x_hbm, a_hbm, wbc_hbm, dec_hbm, skip_hbm, wout_hbm, out_ref,
    xin, ain, din, skip, wb0, blk0, blk1, dsend, dall,
    scale_e, scale_w, scale_x, scale_f, aperm,
    send_x, buf_x, send_a, buf_a, send_k, buf_k, send_g, buf_g,
    send_b, buf_b, send_c, buf_c, send_d, buf_d, send_e, buf_e,
    tmp, xs, res, lsem, ssem, rsem,
):
    b, c = lax.axis_index("frames"), lax.axis_index("mp")
    core = lax.rem(b, 2)
    cy, cx = c // SIDE, lax.rem(c, SIDE)
    scans = b < USED

    loads = {}

    def load(name, src, dst):
        loads[name] = pltpu.make_async_copy(src, dst, lsem.at[len(loads)])
        loads[name].start()

    load("x", x_hbm, xin)
    load("wb0", wbc_hbm.at[0], wb0.at[cy, cx])
    load("dec", dec_hbm, din)
    load("a", a_hbm, ain)
    load("skip", skip_hbm, skip)
    load("out0", wout_hbm.at[0], blk0.at[cy, cx, :, :, pl.ds(0, WIDE)])
    load("bc1", wbc_hbm.at[1], blk0.at[cy, cx, :, :, pl.ds(WIDE, PAIR)])
    load("out1", wout_hbm.at[1], blk1.at[cy, cx])

    def at(axis, peer):
        return (b, peer) if axis == "mp" else (peer, c)

    def peers(axis, act):
        me = c if axis == "mp" else b

        def one(k, carry):
            act(lax.rem(me + k, G))
            return carry

        lax.fori_loop(1, G, one, 0)

    names = []

    def number(name):
        if name not in names:
            names.append(name)
        return names.index(name)

    def copy(name, src, dst, device):
        return pltpu.make_async_remote_copy(
            src_ref=src,
            dst_ref=dst,
            send_sem=ssem.at[number(name)],
            recv_sem=rsem.at[number(name)],
            device_id=device,
            device_id_type=MESH,
        )

    def wait_bytes(sem, name, ref):
        pltpu.make_async_copy(ref, ref, sem.at[number(name)]).wait()

    drains = []

    def send(axis, name, src, dst):
        me = c if axis == "mp" else b
        peers(axis, lambda peer: copy(name, src(peer), dst.at[me], at(axis, peer)).start())
        drains.append(lambda: wait_bytes(ssem, name, dst.at[pl.ds(0, G - 1)]))

    def send_used(name, src, dst):
        def act(peer):
            @pl.when(peer < USED)
            def _():
                copy(name, src(peer), dst.at[b], (peer, c)).start()

        peers("frames", act)

        def drain():
            @pl.when(scans)
            def _():
                wait_bytes(ssem, name, dst.at[pl.ds(0, USED - 1)])

            @pl.when(jnp.logical_not(scans))
            def _():
                wait_bytes(ssem, name, dst.at[pl.ds(0, USED)])

        drains.append(drain)

    def arrived(name, dst):
        wait_bytes(rsem, name, dst.at[pl.ds(0, G - 1)])

    barrier = pltpu.get_barrier_semaphore()
    for axis in ("frames", "mp"):
        peers(
            axis,
            lambda peer, axis=axis: pl.semaphore_signal(
                barrier, inc=1, device_id=at(axis, peer), device_id_type=MESH
            ),
        )

    loads["x"].wait()
    for pair in range(G):
        if pair < USED:
            even = xin[2 * pair].astype(F32)
            odd = xin[2 * pair + 1].astype(F32) if 2 * pair + 1 < JOINTS else jnp.zeros_like(even)
            tmp[0, pl.ds(pair * G, G)] = jnp.concatenate([even, odd], axis=1)
        else:
            tmp[0, pl.ds(pair * G, G)] = jnp.zeros((G, PAIR), F32)
    for frame in range(G):
        send_x[frame] = tmp[0, pl.ds(frame, G, stride=G), :].astype(BF16)
    loads["dec"].wait()
    dsend[...] = jnp.concatenate([din[0], din[1]], axis=1)
    loads["a"].wait()
    row = lax.broadcasted_iota(jnp.int32, (2 * G, JOINTS), 0)
    pick = (lax.broadcasted_iota(jnp.int32, (2 * G, JOINTS), 1) == 2 * lax.rem(row, G) + row // G).astype(F32)
    for layer in range(LAYERS):
        half = jnp.dot(pick, ain[layer], precision=HI, preferred_element_type=F32)
        aperm[layer] = lax.dot_general(
            half, pick, (((1,), (1,)), ((), ())), precision=HI, preferred_element_type=F32
        )
    for name in ("wb0", "skip", "out0", "bc1", "out1"):
        loads[name].wait()
    for layer in range(LAYERS):
        buf_c[layer, pl.ds(USED, G - USED)] = jnp.zeros((G - USED, G, PAIR), BF16)
    buf_x[c] = send_x[c]
    dall[b] = dsend[...]

    pl.semaphore_wait(barrier, 2 * (G - 1))

    send("mp", "x", lambda peer: send_x.at[peer], buf_x)
    peers("mp", lambda peer: copy("wb0", wb0.at[cy, cx], wb0.at[cy, cx], at("mp", peer)).start())

    def wait_wb0(sem):
        wait_bytes(sem, "wb0", flat_wb0)

    flat_wb0 = wb0.reshape(G, 2, HALF // 2, PAIR).at[pl.ds(0, G - 1)]
    drains.append(lambda: wait_wb0(ssem))
    send("frames", "dec", lambda peer: dsend, dall)

    blocks = (blk0, blk1)

    def step1(n):
        blk = blocks[n]
        for i in range(1, SIDE):
            to = lax.rem(cy + i * core, SIDE) * SIDE + lax.rem(cx + i * (1 - core), SIDE)
            part = blk.at[cy, cx, core]
            copy(f"one{n}", part, part, (b, to)).start()
        drains.append(lambda: wait_bytes(ssem, f"one{n}", blk.at[0, pl.ds(0, SIDE - 1), 0]))

    def step2(n):
        blk = blocks[n]
        wait_bytes(rsem, f"one{n}", blk.at[0, pl.ds(0, SIDE - 1), 0])

        @pl.when(core == 0)
        def _():
            for i in range(1, SIDE):
                part = blk.at[cy, :, 0]
                copy(f"two{n}", part, part, (b, lax.rem(cy + i, SIDE) * SIDE + cx)).start()

        @pl.when(core == 1)
        def _():
            for i in range(1, SIDE):
                part = blk.at[:, cx, 1]
                copy(f"two{n}", part, part, (b, cy * SIDE + lax.rem(cx + i, SIDE))).start()

        drains.append(lambda: wait_bytes(ssem, f"two{n}", blk.at[pl.ds(0, SIDE - 1), :, 0]))

    def step3(n):
        blk = blocks[n]
        wait_bytes(rsem, f"two{n}", blk.at[pl.ds(0, SIDE - 1), :, 0])
        part = blk.at[:, :, core]
        copy(f"three{n}", part, part, (b + 1 - 2 * core, c)).start()
        drains.append(lambda: wait_bytes(ssem, f"three{n}", blk.at[:, :, 0]))

    def step4(n):
        wait_bytes(rsem, f"three{n}", blocks[n].at[:, :, 0])

    for n in range(2):
        step1(n)

    def spread(buf, dst):
        for q in range(G // 2):
            even, odd = mix_halves(buf[2 * q].astype(F32), buf[2 * q + 1].astype(F32))
            lanes = pl.ds(q * PAIR, PAIR)
            dst[pl.ds(0, G), lanes] = even.astype(dst.dtype)
            dst[pl.ds(G, G), lanes] = odd.astype(dst.dtype)

    def decay_scales():
        arrived("dec", dall)
        a = dall[...].reshape(FRAMES, PAIR)
        later = lax.broadcasted_iota(jnp.int32, (FRAMES, FRAMES), 0)
        earlier = lax.broadcasted_iota(jnp.int32, (FRAMES, FRAMES), 1)
        logs = jnp.dot(
            (earlier <= later).astype(F32), jnp.log(a), precision=HI, preferred_element_type=F32
        )
        for l in range(LAYERS):
            left = left_half((FRAMES, PAIR))
            mine = left if l == 0 else jnp.logical_not(left)
            la = jnp.where(mine, logs, pltpu.roll(logs, HALF, 1))
            da = 1.0 - jnp.where(mine, a, pltpu.roll(a, HALF, 1))
            for t in range(FRAMES // CHUNK):
                rows = slice(t * CHUNK, (t + 1) * CHUNK)
                rel = la[rows] - la[t * CHUNK + CHUNK // 2 - 1 : t * CHUNK + CHUNK // 2]
                scale_e[l, pl.ds(t * CHUNK, CHUNK)] = jnp.exp(rel)
                scale_w[l, pl.ds(t * CHUNK, CHUNK)] = da[rows] * jnp.exp(-rel)
            end = la[CHUNK - 1 : CHUNK]
            scale_x[l] = da[:CHUNK] * jnp.exp(end - la[:CHUNK])
            scale_f[l] = jnp.exp(la[CHUNK:] - end)

    arrived("x", buf_x)
    spread(buf_x, xs)

    for layer in range(LAYERS):

        def named(name, layer=layer):
            return f"{name}{layer}"

        mixed32 = jnp.dot(aperm[layer], xs[...], precision=HI, preferred_element_type=F32)
        mixed = mixed32.astype(BF16)
        mixed32 = mixed.astype(F32)
        for q in range(G // 2):
            lanes = slice(q * PAIR, (q + 1) * PAIR)
            pieces = mix_halves(mixed32[:G, lanes], mixed32[G:, lanes])
            for i in range(2):
                send_a[layer, 2 * q + i] = pieces[i].astype(BF16)
        send("mp", named("a"), lambda peer: send_a.at[layer, peer], buf_a.at[layer])
        buf_a[layer, c] = send_a[layer, c]
        if layer == 0:
            wait_wb0(rsem)
            weights = wb0[...].reshape(WIDE, PAIR)
        else:
            weights = blk0[:, :, :, :, pl.ds(WIDE, PAIR)].reshape(WIDE, PAIR)
        coef = jnp.dot(mixed, weights, preferred_element_type=F32)
        in_b, out_c = mix_halves(coef[:G], coef[G:])
        for pair in range(USED):
            send_k[layer, pair, :, pl.ds(0, PAIR)] = in_b[pair : pair + 1]
            send_k[layer, pair, :, pl.ds(PAIR, PAIR)] = out_c[pair : pair + 1]
        send_used(named("k"), lambda peer: send_k.at[layer, peer], buf_k.at[layer])

        arrived(named("a"), buf_a.at[layer])
        tmp[0] = buf_a[layer].reshape(FRAMES, PAIR).astype(F32)
        for pair in range(USED):
            send_b[layer, pair] = tmp[0, pl.ds(pair, G, stride=G), :].astype(BF16)
        send_used(named("b"), lambda peer: send_b.at[layer, peer], buf_b.at[layer])

        @pl.when(scans)
        def _():
            buf_b[layer, b] = send_b[layer, b]
            buf_k[layer, b] = send_k[layer, b]
            arrived(named("k"), buf_k.at[layer])
            for block in range(G):
                for part in range(2):
                    tmp[1 + part, pl.ds(block, 1)] = buf_k[layer, block, :, pl.ds(part * PAIR, PAIR)]
            for part in range(2):
                send_g[layer, :, pl.ds(part * PAIR, PAIR)] = tmp[1 + part, pl.ds(0, G)].astype(BF16)
            peers(
                "mp",
                lambda peer: copy(
                    named("g"), send_g.at[layer], buf_g.at[layer, c], (b, peer)
                ).start(),
            )
            buf_g[layer, c] = send_g[layer]

        def drain_g(layer=layer):
            @pl.when(scans)
            def _():
                wait_bytes(ssem, f"g{layer}", buf_g.at[layer, pl.ds(0, G - 1)])

        drains.append(drain_g)
        step2(layer)
        if layer == 0:
            decay_scales()

        @pl.when(scans)
        def _():
            arrived(named("g"), buf_g.at[layer])
            for part in range(2):
                tmp[1 + part] = buf_g[layer, :, :, pl.ds(part * PAIR, PAIR)].reshape(FRAMES, PAIR).astype(F32)
            bp, cp = [
                jnp.concatenate([tmp[1 + part, pl.ds(k, G, stride=G), :] for k in range(G)], axis=0)
                for part in range(2)
            ]
            bp = bp.astype(BF16)
            left = left_half((FRAMES, PAIR))
            causal = lax.broadcasted_iota(jnp.int32, (CHUNK, CHUNK), 1) <= lax.broadcasted_iota(
                jnp.int32, (CHUNK, CHUNK), 0
            )

            def grid(cj, bj, masked):
                g = lax.dot_general(
                    cj, bj, (((1,), (1,)), ((), ())), preferred_element_type=F32
                )
                return (jnp.where(causal, g, 0.0) if masked else g).astype(BF16)

            grids = []
            for j in range(2):
                cj = jnp.where(left if j == 0 else jnp.logical_not(left), cp, 0.0).astype(BF16)
                grids.append(
                    (
                        grid(cj[:CHUNK], bp[:CHUNK], True),
                        grid(cj[CHUNK:], bp[CHUNK:], True),
                        grid(cj[CHUNK:], bp[:CHUNK], False),
                    )
                )
            arrived(named("b"), buf_b.at[layer])
            m = buf_b[layer].reshape(FRAMES, PAIR).astype(F32)
            v = (m * scale_w[layer]).astype(BF16)
            vx = (m[:CHUNK] * scale_x[layer]).astype(BF16)
            values = (v[:CHUNK], v[CHUNK:], vx)
            y0, y1, yx = [
                jnp.where(
                    left[:CHUNK],
                    jnp.dot(grids[0][i], values[i], preferred_element_type=F32),
                    jnp.dot(grids[1][i], values[i], preferred_element_type=F32),
                )
                for i in range(3)
            ]
            gain = skip[pl.ds(layer, 1), :]
            gain = jnp.concatenate([gain, gain], axis=1)
            low = y0 * scale_e[layer, pl.ds(0, CHUNK)] + gain * m[:CHUNK]
            high = (
                y1 * scale_e[layer, pl.ds(CHUNK, CHUNK)] + yx * scale_f[layer] + gain * m[CHUNK:]
            )
            send_c[layer, pl.ds(0, G // 2)] = low.astype(BF16).reshape(G // 2, G, PAIR)
            send_c[layer, pl.ds(G // 2, G // 2)] = high.astype(BF16).reshape(G // 2, G, PAIR)
            peers(
                "frames",
                lambda peer: copy(
                    named("c"), send_c.at[layer, peer], buf_c.at[layer, b], (peer, c)
                ).start(),
            )
            buf_c[layer, b] = send_c[layer, b]

        def drain_c(layer=layer):
            @pl.when(scans)
            def _():
                wait_bytes(ssem, f"c{layer}", buf_c.at[layer, pl.ds(0, G - 1)])

        drains.append(drain_c)
        step3(layer)

        @pl.when(scans)
        def _():
            wait_bytes(rsem, named("c"), buf_c.at[layer, pl.ds(0, USED - 1)])

        @pl.when(jnp.logical_not(scans))
        def _():
            wait_bytes(rsem, named("c"), buf_c.at[layer, pl.ds(0, USED)])

        tmp[0] = buf_c[layer].reshape(FRAMES, PAIR).astype(F32)
        for frame in range(G):
            send_d[layer, frame] = tmp[0, pl.ds(frame, G, stride=G), :].astype(BF16)
        send("mp", named("d"), lambda peer: send_d.at[layer, peer], buf_d.at[layer])
        buf_d[layer, c] = send_d[layer, c]

        step4(layer)
        arrived(named("d"), buf_d.at[layer])
        spread(buf_d.at[layer], res)
        weights = blocks[layer][:, :, :, :, pl.ds(0, WIDE)].reshape(WIDE, WIDE)
        xs[...] += jnp.dot(res[...], weights, preferred_element_type=F32)

    for q in range(G // 2):
        lanes = pl.ds(q * PAIR, PAIR)
        pieces = mix_halves(xs[pl.ds(0, G), lanes], xs[pl.ds(G, G), lanes])
        send_e[2 * q] = pieces[0]
        send_e[2 * q + 1] = pieces[1]
    send("mp", "e", lambda peer: send_e.at[peer], buf_e)
    buf_e[c] = send_e[c]
    for drain in drains:
        drain()
    arrived("e", buf_e)
    tmp[0] = buf_e[...].reshape(FRAMES, PAIR)
    for pair in range(USED):
        both = tmp[0, pl.ds(pair, G, stride=G), :]
        out_ref[2 * pair] = both[:, :HALF]
        if 2 * pair + 1 < JOINTS:
            out_ref[2 * pair + 1] = both[:, HALF:]


def shards(motion, adjacency, w_bc, decay, skip, w_out):
    vm = pltpu.VMEM
    part = HALF // 2
    out = pl.pallas_call(
        body,
        out_shape=jax.ShapeDtypeStruct((JOINTS, G, HALF), F32),
        in_specs=[pl.BlockSpec(memory_space=pltpu.HBM)] * 6,
        out_specs=pl.BlockSpec(memory_space=vm),
        scratch_shapes=[
            vm((JOINTS, G, HALF), BF16),
            vm((LAYERS, JOINTS, JOINTS), F32),
            vm((LAYERS, G, HALF), F32),
            vm((LAYERS, HALF), F32),
            vm((SIDE, SIDE, 2, part, PAIR), BF16),
            vm((SIDE, SIDE, 2, part, WIDE + PAIR), BF16),
            vm((SIDE, SIDE, 2, part, WIDE), BF16),
            vm((G, PAIR), F32),
            vm((G, G, PAIR), F32),
            vm((LAYERS, FRAMES, PAIR), F32),
            vm((LAYERS, FRAMES, PAIR), F32),
            vm((LAYERS, CHUNK, PAIR), F32),
            vm((LAYERS, CHUNK, PAIR), F32),
            vm((LAYERS, 2 * G, 2 * G), F32),
            vm((G, G, PAIR), BF16),
            vm((G, G, PAIR), BF16),
            vm((LAYERS, G, G, PAIR), BF16),
            vm((LAYERS, G, G, PAIR), BF16),
            vm((LAYERS, USED, 1, 2 * PAIR), F32),
            vm((LAYERS, G, 1, 2 * PAIR), F32),
            vm((LAYERS, G, 2 * PAIR), BF16),
            vm((LAYERS, G, G, 2 * PAIR), BF16),
            vm((LAYERS, USED, G, PAIR), BF16),
            vm((LAYERS, G, G, PAIR), BF16),
            vm((LAYERS, G, G, PAIR), BF16),
            vm((LAYERS, G, G, PAIR), BF16),
            vm((LAYERS, G, G, PAIR), BF16),
            vm((LAYERS, G, G, PAIR), BF16),
            vm((G, G, PAIR), F32),
            vm((G, G, PAIR), F32),
            vm((3, FRAMES, PAIR), F32),
            vm((2 * G, WIDE), F32),
            vm((2 * G, WIDE), BF16),
            pltpu.SemaphoreType.DMA((8,)),
            pltpu.SemaphoreType.DMA((24,)),
            pltpu.SemaphoreType.DMA((24,)),
        ],
        compiler_params=pltpu.CompilerParams(
            collective_id=0, has_side_effects=True, vmem_limit_bytes=40 * 2**20
        ),
    )(
        motion.transpose(1, 0, 2),
        adjacency,
        w_bc.reshape(LAYERS, 2, part, PAIR),
        decay,
        skip,
        w_out.reshape(LAYERS, 2, part, WIDE),
    )
    return out.transpose(1, 0, 2)


def solution(mesh):
    return jax.shard_map(
        shards,
        mesh=mesh,
        in_specs=(
            P("frames", None, "mp"),
            P(),
            P(None, "mp", None),
            P(None, "frames", "mp"),
            P(None, "mp"),
            P(None, "mp", None),
        ),
        out_specs=P("frames", None, "mp"),
        check_vma=False,
    )
```

time: 582 us -> 72.7 us (0.12)
  waiting for transfers between devices: 460 us -> 0 us
  Pallas kernels: 0 us -> 69.2 us
  other arithmetic: 40.9 us -> 0 us
  blocking collectives: 39.4 us -> 0 us
  matrix products: 14.6 us -> 0 us
  between operations: 13.8 us -> 0.03 us
  local copies, waits for them, and re-layouts: 9.76 us -> 3.31 us
    psum x2 -> x0, waiting for transfers between devices: 190 us -> none  [shards(): coef = lax.psum(partial_coef, 'mp').reshape(frames_loc, joints, 2 * state)]
    unnamed x8 -> x0, waiting for transfers between devices: 152 us -> none
    all_gather x2 -> x0, waiting for transfers between devices: 118 us -> none  [entering(): pieces = jax.tree.map(lambda part: lax.all_gather(part, axis), value)]
    pallas_call x0 -> x1, Pallas kernels: none -> 69.2 us  [shards(): pl.pallas_call(body, out_shape=jax.ShapeDtypeStruct((JOINTS, G, HALF), F3...]
    select_n x30 -> x0, other arithmetic: 40.7 us -> none  [lap(): jnp.where(position < mine, new, old)]
    all_gather x2 -> x0, blocking collectives: 39.4 us -> none  [entering(): pieces = jax.tree.map(lambda part: lax.all_gather(part, axis), value)]
    dot_general x14 -> x0, matrix products: 14.6 us -> none  [the longest x2 6.74 us: shards(): jnp.einsum('sjd,sjn->jdn', weighted * total[None, None, :], in_b, precisi...]
  transfers between devices with their start and end apart: 6 -> 0, of which waited for: 6 -> 0; matrix products, arithmetic and copies ran while one was open for 0% -> 0% of each run, Pallas kernels for 0% -> 0%
where the time goes in v2:
time: 72.7 us; the launch traced here: 72.5 us
  Pallas kernels  69.2 us (95%)
  local copies, waits for them, and re-layouts  3.31 us (5%)
    pallas_call x1, Pallas kernels, shards(): pl.pallas_call(body, out_shape=jax.ShapeDtypeStruct((JOINTS, G, HALF), F3...  69.2 us
    unnamed x12, local copies, waits for them, and re-layouts  3.31 us

profile of v2, /device:TPU:1, one launch (start us, length us, event | category | flops | bytes accessed | tf_op | source)
XLA Modules:
  0.0 72.5 jit_solution(11806653604161503669)
XLA Ops:
  0.0 0.0 copy-start.2
  0.0 0.0 copy-start.3
  0.0 0.0 copy-start.4
  0.0 0.8 %copy.7.a_hbm = f32[2,25,25]{2,1,0:T(8,128)S(1)} copy(f32[2,25,25]{2,0,1:T(2,128)} %param.7) | data formatting | bytes 10000 | tf_op args[1]
  0.8 0.0 copy-done.2
  0.8 0.0 copy-done.3
  0.8 0.0 copy-done.4
  0.8 0.0 copy-start
  0.8 0.9 %copy-done = bf16[2,64,1024]{2,1,0:T(8,128)(2,1)S(1)} copy-done((bf16[2,64,1024]{2,1,0:T(8,128)(2,1)S(1)}, bf16[2,64,1024]{2,1,0:T(8,128)(2,1)}, u32[]{:S(2)}) %copy-start) | copy-done | bytes 262168
  1.8 0.0 copy-start.1
  1.8 0.9 %copy-done.1 = bf16[16,25,64]{2,0,1:T(8,128)(2,1)S(1)} copy-done((bf16[16,25,64]{2,0,1:T(8,128)(2,1)S(1)}, bf16[16,25,64]{2,0,1:T(8,128)(2,1)}, u32[]{:S(2)}) %copy-start.1) | copy-done | bytes 51224
  2.6 69.2 %shard_map.64 = f32[25,16,64]{2,1,0:T(8,128)S(1)} custom-call(bf16[25,16,64]{2,1,0:T(8,128)(2,1)S(1)} %bitcast.6, f32[2,25,25]{2,1,0:T(8,128)S(1)} %copy.7.a_hbm, bf16[2,2,32,128]{3,2,1,0:T(8,128)(2,1)S(1)} %bitcast.7, f32[2,16,64]{2,1,0:T(8,128)S(1)} %copy-done.3, f32[2,64]{1,0:T(2,128)S(1)} %copy-done.4, bf16[2,2,32,1024]{3,2,1,0:T(8,128)(2,1)S(1)} %bitcast.5), custom_call_target="tpu_custom_call" | custom-call | tf_op jit(solution)/shard_map/pallas_call | solution.py:414
  71.8 0.7 copy.9
Async XLA Ops:
  0.0 0.8 %copy-start.2 = (bf16[2,64,128]{2,1,0:T(8,128)(2,1)S(1)}, bf16[2,64,128]{2,1,0:T(8,128)(2,1)}, u32[]{:S(2)}) copy-start(bf16[2,64,128]{2,1,0:T(8,128)(2,1)} %param.8) | copy-start | bytes 98308
  0.0 0.8 %copy-start.3 = (f32[2,16,64]{2,1,0:T(8,128)S(1)}, f32[2,16,64]{2,1,0:T(8,128)}, u32[]{:S(2)}) copy-start(f32[2,16,64]{2,1,0:T(8,128)} %dec_hbm.1) | copy-start | bytes 24580
  0.0 0.8 %copy-start.4 = (f32[2,64]{1,0:T(2,128)S(1)}, f32[2,64]{1,0:T(2,128)}, u32[]{:S(2)}) copy-start(f32[2,64]{1,0:T(2,128)} %skip_hbm.1) | copy-start | bytes 1540
  0.8 1.0 %copy-start = (bf16[2,64,1024]{2,1,0:T(8,128)(2,1)S(1)}, bf16[2,64,1024]{2,1,0:T(8,128)(2,1)}, u32[]{:S(2)}) copy-start(bf16[2,64,1024]{2,1,0:T(8,128)(2,1)} %param.11) | copy-start | bytes 786436
  1.8 0.9 %copy-start.1 = (bf16[16,25,64]{2,0,1:T(8,128)(2,1)S(1)}, bf16[16,25,64]{2,0,1:T(8,128)(2,1)}, u32[]{:S(2)}) copy-start(bf16[16,25,64]{2,0,1:T(8,128)(2,1)} %param.6) | copy-start | bytes 153604

commit v3 on v2

--- a/solution.py
+++ b/solution.py
@@ -33,7 +33,7 @@
 
 def body(
     x_hbm, a_hbm, wbc_hbm, dec_hbm, skip_hbm, wout_hbm, out_ref,
-    xin, ain, din, skip, wb0, blk0, blk1, dsend, dall,
+    xin, araw, ain, din, skip, wb0, blk0, blk1, dsend, dall,
     scale_e, scale_w, scale_x, scale_f, aperm,
     send_x, buf_x, send_a, buf_a, send_k, buf_k, send_g, buf_g,
     send_b, buf_b, send_c, buf_c, send_d, buf_d, send_e, buf_e,
@@ -53,23 +53,29 @@
     load("x", x_hbm, xin)
     load("wb0", wbc_hbm.at[0], wb0.at[cy, cx])
     load("dec", dec_hbm, din)
-    load("a", a_hbm, ain)
+    load("a", a_hbm, araw)
     load("skip", skip_hbm, skip)
-    load("out0", wout_hbm.at[0], blk0.at[cy, cx, :, :, pl.ds(0, WIDE)])
-    load("bc1", wbc_hbm.at[1], blk0.at[cy, cx, :, :, pl.ds(WIDE, PAIR)])
-    load("out1", wout_hbm.at[1], blk1.at[cy, cx])
+    load("out0", wout_hbm.at[0, core], blk0.at[cy, cx, core, :, pl.ds(0, WIDE)])
+    load("bc1", wbc_hbm.at[1, core], blk0.at[cy, cx, core, :, pl.ds(WIDE, PAIR)])
+    load("out1", wout_hbm.at[1, core], blk1.at[cy, cx, core])
 
     def at(axis, peer):
         return (b, peer) if axis == "mp" else (peer, c)
 
     def peers(axis, act):
-        me = c if axis == "mp" else b
+        def off(k, half):
+            return half + (k + 1) // 2 * (1 - 2 * lax.rem(k + 1, 2))
 
         def one(k, carry):
-            act(lax.rem(me + k, G))
+            if axis == "mp":
+                to_y = lax.rem(cy + off(k // SIDE, SIDE // 2), SIDE)
+                to_x = lax.rem(cx + off(lax.rem(k, SIDE), SIDE // 2), SIDE)
+                act(to_y * SIDE + to_x)
+            else:
+                act(lax.rem(b + off(k, G // 2), G))
             return carry
 
-        lax.fori_loop(1, G, one, 0)
+        lax.fori_loop(0, G - 1, one, 0)
 
     names = []
 
@@ -139,9 +145,23 @@
             tmp[0, pl.ds(pair * G, G)] = jnp.zeros((G, PAIR), F32)
     for frame in range(G):
         send_x[frame] = tmp[0, pl.ds(frame, G, stride=G), :].astype(BF16)
+    buf_x[c] = send_x[c]
+
+    pl.semaphore_wait(barrier, 2 * (G - 1))
+
+    send("mp", "x", lambda peer: send_x.at[peer], buf_x)
+    loads["wb0"].wait()
+    peers("mp", lambda peer: copy("wb0", wb0.at[cy, cx], wb0.at[cy, cx], at("mp", peer)).start())
+    flat_wb0 = wb0.reshape(G, 2, HALF // 2, PAIR).at[pl.ds(0, G - 1)]
+    drains.append(lambda: wait_bytes(ssem, "wb0", flat_wb0))
     loads["dec"].wait()
     dsend[...] = jnp.concatenate([din[0], din[1]], axis=1)
+    send("frames", "dec", lambda peer: dsend, dall)
+    dall[b] = dsend[...]
     loads["a"].wait()
+    for joint in range(JOINTS):
+        for layer in range(LAYERS):
+            ain[layer, pl.ds(joint, 1)] = araw[joint, pl.ds(layer, 1)]
     row = lax.broadcasted_iota(jnp.int32, (2 * G, JOINTS), 0)
     pick = (lax.broadcasted_iota(jnp.int32, (2 * G, JOINTS), 1) == 2 * lax.rem(row, G) + row // G).astype(F32)
     for layer in range(LAYERS):
@@ -149,24 +169,9 @@
         aperm[layer] = lax.dot_general(
             half, pick, (((1,), (1,)), ((), ())), precision=HI, preferred_element_type=F32
         )
-    for name in ("wb0", "skip", "out0", "bc1", "out1"):
+        buf_c[layer, pl.ds(USED, G - USED)] = jnp.zeros((G - USED, G, PAIR), BF16)
+    for name in ("skip", "out0", "bc1", "out1"):
         loads[name].wait()
-    for layer in range(LAYERS):
-        buf_c[layer, pl.ds(USED, G - USED)] = jnp.zeros((G - USED, G, PAIR), BF16)
-    buf_x[c] = send_x[c]
-    dall[b] = dsend[...]
-
-    pl.semaphore_wait(barrier, 2 * (G - 1))
-
-    send("mp", "x", lambda peer: send_x.at[peer], buf_x)
-    peers("mp", lambda peer: copy("wb0", wb0.at[cy, cx], wb0.at[cy, cx], at("mp", peer)).start())
-
-    def wait_wb0(sem):
-        wait_bytes(sem, "wb0", flat_wb0)
-
-    flat_wb0 = wb0.reshape(G, 2, HALF // 2, PAIR).at[pl.ds(0, G - 1)]
-    drains.append(lambda: wait_wb0(ssem))
-    send("frames", "dec", lambda peer: dsend, dall)
 
     blocks = (blk0, blk1)
 
@@ -184,21 +189,39 @@
 
         @pl.when(core == 0)
         def _():
-            for i in range(1, SIDE):
+            for i in (1, SIDE - 1):
                 part = blk.at[cy, :, 0]
                 copy(f"two{n}", part, part, (b, lax.rem(cy + i, SIDE) * SIDE + cx)).start()
 
         @pl.when(core == 1)
         def _():
-            for i in range(1, SIDE):
+            for i in (1, SIDE - 1):
                 part = blk.at[:, cx, 1]
                 copy(f"two{n}", part, part, (b, cy * SIDE + lax.rem(cx + i, SIDE))).start()
 
-        drains.append(lambda: wait_bytes(ssem, f"two{n}", blk.at[pl.ds(0, SIDE - 1), :, 0]))
+        drains.append(lambda: wait_bytes(ssem, f"two{n}", blk.at[pl.ds(0, 2), :, 0]))
+
+    def step2b(n):
+        blk = blocks[n]
+        wait_bytes(rsem, f"two{n}", blk.at[pl.ds(0, 2), :, 0])
+
+        @pl.when(core == 0)
+        def _():
+            for i in (1, SIDE - 1):
+                part = blk.at[lax.rem(cy + SIDE - i, SIDE), pl.ds(i // 2 * 2, 2), 0]
+                copy(f"far{n}", part, part, (b, lax.rem(cy + i, SIDE) * SIDE + cx)).start()
+
+        @pl.when(core == 1)
+        def _():
+            for i in (1, SIDE - 1):
+                part = blk.at[pl.ds(i // 2 * 2, 2), lax.rem(cx + SIDE - i, SIDE), 1]
+                copy(f"far{n}", part, part, (b, cy * SIDE + lax.rem(cx + i, SIDE))).start()
+
+        drains.append(lambda: wait_bytes(ssem, f"far{n}", blk.at[0, :, 0]))
 
     def step3(n):
         blk = blocks[n]
-        wait_bytes(rsem, f"two{n}", blk.at[pl.ds(0, SIDE - 1), :, 0])
+        wait_bytes(rsem, f"far{n}", blk.at[0, :, 0])
         part = blk.at[:, :, core]
         copy(f"three{n}", part, part, (b + 1 - 2 * core, c)).start()
         drains.append(lambda: wait_bytes(ssem, f"three{n}", blk.at[:, :, 0]))
@@ -206,8 +229,7 @@
     def step4(n):
         wait_bytes(rsem, f"three{n}", blocks[n].at[:, :, 0])
 
-    for n in range(2):
-        step1(n)
+    step1(0)
 
     def spread(buf, dst):
         for q in range(G // 2):
@@ -257,7 +279,7 @@
         send("mp", named("a"), lambda peer: send_a.at[layer, peer], buf_a.at[layer])
         buf_a[layer, c] = send_a[layer, c]
         if layer == 0:
-            wait_wb0(rsem)
+            wait_bytes(rsem, "wb0", flat_wb0)
             weights = wb0[...].reshape(WIDE, PAIR)
         else:
             weights = blk0[:, :, :, :, pl.ds(WIDE, PAIR)].reshape(WIDE, PAIR)
@@ -268,6 +290,8 @@
             send_k[layer, pair, :, pl.ds(PAIR, PAIR)] = out_c[pair : pair + 1]
         send_used(named("k"), lambda peer: send_k.at[layer, peer], buf_k.at[layer])
 
+        if layer == 0:
+            step2(0)
         arrived(named("a"), buf_a.at[layer])
         tmp[0] = buf_a[layer].reshape(FRAMES, PAIR).astype(F32)
         for pair in range(USED):
@@ -298,7 +322,10 @@
                 wait_bytes(ssem, f"g{layer}", buf_g.at[layer, pl.ds(0, G - 1)])
 
         drains.append(drain_g)
-        step2(layer)
+        if layer == 0:
+            step2b(0)
+        if layer == 1:
+            step2b(1)
         if layer == 0:
             decay_scales()
 
@@ -368,7 +395,12 @@
                 wait_bytes(ssem, f"c{layer}", buf_c.at[layer, pl.ds(0, G - 1)])
 
         drains.append(drain_c)
-        step3(layer)
+        if layer == 0:
+            step3(0)
+        if layer == 0:
+            step1(1)
+        if layer == 1:
+            step3(1)
 
         @pl.when(scans)
         def _():
@@ -383,8 +415,13 @@
             send_d[layer, frame] = tmp[0, pl.ds(frame, G, stride=G), :].astype(BF16)
         send("mp", named("d"), lambda peer: send_d.at[layer, peer], buf_d.at[layer])
         buf_d[layer, c] = send_d[layer, c]
-
-        step4(layer)
+        if layer == 0:
+            step2(1)
+
+        if layer == 0:
+            step4(0)
+        if layer == 1:
+            step4(1)
         arrived(named("d"), buf_d.at[layer])
         spread(buf_d.at[layer], res)
         weights = blocks[layer][:, :, :, :, pl.ds(0, WIDE)].reshape(WIDE, WIDE)
@@ -400,12 +437,7 @@
     for drain in drains:
         drain()
     arrived("e", buf_e)
-    tmp[0] = buf_e[...].reshape(FRAMES, PAIR)
-    for pair in range(USED):
-        both = tmp[0, pl.ds(pair, G, stride=G), :]
-        out_ref[2 * pair] = both[:, :HALF]
-        if 2 * pair + 1 < JOINTS:
-            out_ref[2 * pair + 1] = both[:, HALF:]
+    out_ref[...] = buf_e[...]
 
 
 def shards(motion, adjacency, w_bc, decay, skip, w_out):
@@ -413,11 +445,12 @@
     part = HALF // 2
     out = pl.pallas_call(
         body,
-        out_shape=jax.ShapeDtypeStruct((JOINTS, G, HALF), F32),
+        out_shape=jax.ShapeDtypeStruct((G, G, PAIR), F32),
         in_specs=[pl.BlockSpec(memory_space=pltpu.HBM)] * 6,
         out_specs=pl.BlockSpec(memory_space=vm),
         scratch_shapes=[
             vm((JOINTS, G, HALF), BF16),
+            vm((JOINTS, LAYERS, JOINTS), F32),
             vm((LAYERS, JOINTS, JOINTS), F32),
             vm((LAYERS, G, HALF), F32),
             vm((LAYERS, HALF), F32),
@@ -455,17 +488,17 @@
             pltpu.SemaphoreType.DMA((24,)),
         ],
         compiler_params=pltpu.CompilerParams(
-            collective_id=0, has_side_effects=True, vmem_limit_bytes=40 * 2**20
+            collective_id=0, has_side_effects=True, vmem_limit_bytes=56 * 2**20
         ),
     )(
         motion.transpose(1, 0, 2),
-        adjacency,
+        adjacency.transpose(1, 0, 2),
         w_bc.reshape(LAYERS, 2, part, PAIR),
         decay,
         skip,
         w_out.reshape(LAYERS, 2, part, WIDE),
     )
-    return out.transpose(1, 0, 2)
+    return out.reshape(G, 2 * G, HALF)[:, :JOINTS]
 
 
 def solution(mesh):

time: 72.7 us -> 66.1 us (0.909)
  Pallas kernels: 69.2 us -> 64 us
  local copies, waits for them, and re-layouts: 3.31 us -> 1.81 us
    pallas_call x1, Pallas kernels: 69.2 us -> 64 us  [shards(): pl.pallas_call(body, out_shape=jax.ShapeDtypeStruct((G, G, PAIR), F32), i...]
    unnamed x12 -> x1, local copies, waits for them, and re-layouts: 3.31 us -> 0.8 us
    reshape x0 -> x1, local copies, waits for them, and re-layouts: none -> 1 us  [shards(): return out.reshape(G, 2 * G, HALF)[:, :JOINTS]]
where the time goes in v3:
time: 66.1 us; the launch traced here: 65.8 us
  Pallas kernels  64 us (97%)
  local copies, waits for them, and re-layouts  1.81 us (3%)
    pallas_call x1, Pallas kernels, shards(): pl.pallas_call(body, out_shape=jax.ShapeDtypeStruct((G, G, PAIR), F32), i...  64 us

profile of v3, /device:TPU:1, one launch (start us, length us, event | category | flops | bytes accessed | tf_op | source)
XLA Modules:
  0.0 65.8 jit_solution(11170487357916879439)
XLA Ops:
  0.0 64.0 %shard_map.64 = f32[16,16,128]{2,1,0:T(8,128)} custom-call(bf16[25,16,64]{2,1,0:T(8,128)(2,1)} %bitcast.7, f32[25,2,25]{2,1,0:T(2,128)} %bitcast.9, bf16[2,2,32,128]{3,2,1,0:T(8,128)(2,1)} %bitcast.8, f32[2,16,64]{2,1,0:T(8,128)} %dec_hbm.1, f32[2,64]{1,0:T(2,128)} %skip_hbm.1, bf16[2,2,32,1024]{3,2,1,0:T(8,128)(2,1)} %bitcast.6), custom_call_target="tpu_custom_call" | custom-call | tf_op jit(solution)/shard_map/pallas_call | solution.py:446
  64.0 1.0 %reshape.11 = f32[16,32,64]{2,1,0:T(8,128)S(1)} reshape(f32[16,16,128]{2,1,0:T(8,128)} %shard_map.64) | data formatting | bytes 262144 | tf_op jit(solution)/shard_map/reshape | solution.py:501
  65.0 0.8 %copy.8 = f32[16,25,64]{2,0,1:T(8,128)} copy(f32[16,25,64]{2,1,0:T(8,128)S(1)} %bitcast.5) | data formatting | bytes 204800

commit v4 on v3

--- a/solution.py
+++ b/solution.py
@@ -230,6 +230,7 @@
         wait_bytes(rsem, f"three{n}", blocks[n].at[:, :, 0])
 
     step1(0)
+    step1(1)
 
     def spread(buf, dst):
         for q in range(G // 2):
@@ -278,6 +279,8 @@
                 send_a[layer, 2 * q + i] = pieces[i].astype(BF16)
         send("mp", named("a"), lambda peer: send_a.at[layer, peer], buf_a.at[layer])
         buf_a[layer, c] = send_a[layer, c]
+        if layer == 1:
+            step2(1)
         if layer == 0:
             wait_bytes(rsem, "wb0", flat_wb0)
             weights = wb0[...].reshape(WIDE, PAIR)
@@ -397,8 +400,6 @@
         drains.append(drain_c)
         if layer == 0:
             step3(0)
-        if layer == 0:
-            step1(1)
         if layer == 1:
             step3(1)
 
@@ -415,8 +416,6 @@
             send_d[layer, frame] = tmp[0, pl.ds(frame, G, stride=G), :].astype(BF16)
         send("mp", named("d"), lambda peer: send_d.at[layer, peer], buf_d.at[layer])
         buf_d[layer, c] = send_d[layer, c]
-        if layer == 0:
-            step2(1)
 
         if layer == 0:
             step4(0)

time: 66.1 us -> 65.4 us (0.989)
  no operation moved by 1% of the time
where the time goes in v4:
time: 65.4 us; the launch traced here: 65.2 us
  Pallas kernels  63.4 us (97%)
  local copies, waits for them, and re-layouts  1.81 us (3%)
    pallas_call x1, Pallas kernels, shards(): pl.pallas_call(body, out_shape=jax.ShapeDtypeStruct((G, G, PAIR), F32), i...  63.4 us

profile of v4, /device:TPU:1, one launch (start us, length us, event | category | flops | bytes accessed | tf_op | source)
XLA Modules:
  0.0 65.2 jit_solution(6138752018430831951)
XLA Ops:
  0.0 63.4 %shard_map.64 = f32[16,16,128]{2,1,0:T(8,128)} custom-call(bf16[25,16,64]{2,1,0:T(8,128)(2,1)} %bitcast.7, f32[25,2,25]{2,1,0:T(2,128)} %bitcast.9, bf16[2,2,32,128]{3,2,1,0:T(8,128)(2,1)} %bitcast.8, f32[2,16,64]{2,1,0:T(8,128)} %dec_hbm.1, f32[2,64]{1,0:T(2,128)} %skip_hbm.1, bf16[2,2,32,1024]{3,2,1,0:T(8,128)(2,1)} %bitcast.6), custom_call_target="tpu_custom_call" | custom-call | tf_op jit(solution)/shard_map/pallas_call | solution.py:445
  63.4 1.0 %reshape.11 = f32[16,32,64]{2,1,0:T(8,128)S(1)} reshape(f32[16,16,128]{2,1,0:T(8,128)} %shard_map.64) | data formatting | bytes 262144 | tf_op jit(solution)/shard_map/reshape | solution.py:500
  64.4 0.8 %copy.8 = f32[16,25,64]{2,0,1:T(8,128)} copy(f32[16,25,64]{2,1,0:T(8,128)S(1)} %bitcast.5) | data formatting | bytes 204800

commit v5 on v4

--- a/solution.py
+++ b/solution.py
@@ -51,13 +51,6 @@
         loads[name].start()
 
     load("x", x_hbm, xin)
-    load("wb0", wbc_hbm.at[0], wb0.at[cy, cx])
-    load("dec", dec_hbm, din)
-    load("a", a_hbm, araw)
-    load("skip", skip_hbm, skip)
-    load("out0", wout_hbm.at[0, core], blk0.at[cy, cx, core, :, pl.ds(0, WIDE)])
-    load("bc1", wbc_hbm.at[1, core], blk0.at[cy, cx, core, :, pl.ds(WIDE, PAIR)])
-    load("out1", wout_hbm.at[1, core], blk1.at[cy, cx, core])
 
     def at(axis, peer):
         return (b, peer) if axis == "mp" else (peer, c)
@@ -134,6 +127,14 @@
                 barrier, inc=1, device_id=at(axis, peer), device_id_type=MESH
             ),
         )
+
+    load("wb0", wbc_hbm.at[0], wb0.at[cy, cx])
+    load("dec", dec_hbm, din)
+    load("a", a_hbm, araw)
+    load("skip", skip_hbm, skip)
+    load("out0", wout_hbm.at[0, core], blk0.at[cy, cx, core, :, pl.ds(0, WIDE)])
+    load("bc1", wbc_hbm.at[1, core], blk0.at[cy, cx, core, :, pl.ds(WIDE, PAIR)])
+    load("out1", wout_hbm.at[1, core], blk1.at[cy, cx, core])
 
     loads["x"].wait()
     for pair in range(G):
@@ -351,7 +352,9 @@
                 g = lax.dot_general(
                     cj, bj, (((1,), (1,)), ((), ())), preferred_element_type=F32
                 )
-                return (jnp.where(causal, g, 0.0) if masked else g).astype(BF16)
+                g = jnp.where(causal, g, 0.0) if masked else g
+                first = g.astype(BF16)
+                return jnp.concatenate([first, (g - first.astype(F32)).astype(BF16), first], axis=1)
 
             grids = []
             for j in range(2):
@@ -365,9 +368,13 @@
                 )
             arrived(named("b"), buf_b.at[layer])
             m = buf_b[layer].reshape(FRAMES, PAIR).astype(F32)
-            v = (m * scale_w[layer]).astype(BF16)
-            vx = (m[:CHUNK] * scale_x[layer]).astype(BF16)
-            values = (v[:CHUNK], v[CHUNK:], vx)
+            v = m * scale_w[layer]
+            vx = m[:CHUNK] * scale_x[layer]
+            values = []
+            for p in (v[:CHUNK], v[CHUNK:], vx):
+                first = p.astype(BF16)
+                rest = (p - first.astype(F32)).astype(BF16)
+                values.append(jnp.concatenate([first, first, rest], axis=0))
             y0, y1, yx = [
                 jnp.where(
                     left[:CHUNK],

time: 65.4 us -> 65.4 us (level)
  no operation moved by 1% of the time
where the time goes in v5:
time: 65.4 us; the launch traced here: 65.3 us
  Pallas kernels  63.5 us (97%)
  local copies, waits for them, and re-layouts  1.81 us (3%)
    pallas_call x1, Pallas kernels, shards(): pl.pallas_call(body, out_shape=jax.ShapeDtypeStruct((G, G, PAIR), F32), i...  63.5 us

profile of v5, /device:TPU:1, one launch (start us, length us, event | category | flops | bytes accessed | tf_op | source)
XLA Modules:
  0.0 65.3 jit_solution(6522544078670125213)
XLA Ops:
  0.0 63.5 %shard_map.64 = f32[16,16,128]{2,1,0:T(8,128)} custom-call(bf16[25,16,64]{2,1,0:T(8,128)(2,1)} %bitcast.7, f32[25,2,25]{2,1,0:T(2,128)} %bitcast.9, bf16[2,2,32,128]{3,2,1,0:T(8,128)(2,1)} %bitcast.8, f32[2,16,64]{2,1,0:T(8,128)} %dec_hbm.1, f32[2,64]{1,0:T(2,128)} %skip_hbm.1, bf16[2,2,32,1024]{3,2,1,0:T(8,128)(2,1)} %bitcast.6), custom_call_target="tpu_custom_call" | custom-call | tf_op jit(solution)/shard_map/pallas_call | solution.py:452
  63.5 1.0 %reshape.11 = f32[16,32,64]{2,1,0:T(8,128)S(1)} reshape(f32[16,16,128]{2,1,0:T(8,128)} %shard_map.64) | data formatting | bytes 262144 | tf_op jit(solution)/shard_map/reshape | solution.py:507
  64.5 0.8 %copy.8 = f32[16,25,64]{2,0,1:T(8,128)} copy(f32[16,25,64]{2,1,0:T(8,128)S(1)} %bitcast.5) | data formatting | bytes 204800

commit v6 on v5

--- a/solution.py
+++ b/solution.py
@@ -68,7 +68,7 @@
                 act(lax.rem(b + off(k, G // 2), G))
             return carry
 
-        lax.fori_loop(0, G - 1, one, 0)
+        lax.fori_loop(0, G - 1, one, 0, unroll=3)
 
     names = []
 
@@ -230,8 +230,6 @@
     def step4(n):
         wait_bytes(rsem, f"three{n}", blocks[n].at[:, :, 0])
 
-    step1(0)
-    step1(1)
 
     def spread(buf, dst):
         for q in range(G // 2):
@@ -295,7 +293,8 @@
         send_used(named("k"), lambda peer: send_k.at[layer, peer], buf_k.at[layer])
 
         if layer == 0:
-            step2(0)
+            step1(0)
+            step1(1)
         arrived(named("a"), buf_a.at[layer])
         tmp[0] = buf_a[layer].reshape(FRAMES, PAIR).astype(F32)
         for pair in range(USED):
@@ -327,7 +326,7 @@
 
         drains.append(drain_g)
         if layer == 0:
-            step2b(0)
+            step2(0)
         if layer == 1:
             step2b(1)
         if layer == 0:
@@ -406,7 +405,7 @@
 
         drains.append(drain_c)
         if layer == 0:
-            step3(0)
+            step2b(0)
         if layer == 1:
             step3(1)
 
@@ -425,6 +424,7 @@
         buf_d[layer, c] = send_d[layer, c]
 
         if layer == 0:
+            step3(0)
             step4(0)
         if layer == 1:
             step4(1)
@@ -438,12 +438,11 @@
         pieces = mix_halves(xs[pl.ds(0, G), lanes], xs[pl.ds(G, G), lanes])
         send_e[2 * q] = pieces[0]
         send_e[2 * q + 1] = pieces[1]
-    send("mp", "e", lambda peer: send_e.at[peer], buf_e)
-    buf_e[c] = send_e[c]
+    send("mp", "e", lambda peer: send_e.at[peer], out_ref)
+    out_ref[c] = send_e[c]
     for drain in drains:
         drain()
-    arrived("e", buf_e)
-    out_ref[...] = buf_e[...]
+    arrived("e", out_ref)
 
 
 def shards(motion, adjacency, w_bc, decay, skip, w_out):

time: 65.4 us -> 65 us (level)
  no operation moved by 1% of the time
where the time goes in v6:
time: 65 us; the launch traced here: 64.9 us
  Pallas kernels  63.1 us (97%)
  local copies, waits for them, and re-layouts  1.81 us (3%)
    pallas_call x1, Pallas kernels, shards(): pl.pallas_call(body, out_shape=jax.ShapeDtypeStruct((G, G, PAIR), F32), i...  63.1 us

profile of v6, /device:TPU:1, one launch (start us, length us, event | category | flops | bytes accessed | tf_op | source)
XLA Modules:
  0.0 64.9 jit_solution(1882162798748640061)
XLA Ops:
  0.0 63.1 %shard_map.64 = f32[16,16,128]{2,1,0:T(8,128)} custom-call(bf16[25,16,64]{2,1,0:T(8,128)(2,1)} %bitcast.7, f32[25,2,25]{2,1,0:T(2,128)} %bitcast.9, bf16[2,2,32,128]{3,2,1,0:T(8,128)(2,1)} %bitcast.8, f32[2,16,64]{2,1,0:T(8,128)} %dec_hbm.1, f32[2,64]{1,0:T(2,128)} %skip_hbm.1, bf16[2,2,32,1024]{3,2,1,0:T(8,128)(2,1)} %bitcast.6), custom_call_target="tpu_custom_call" | custom-call | tf_op jit(solution)/shard_map/pallas_call | solution.py:451
  63.1 1.0 %reshape.11 = f32[16,32,64]{2,1,0:T(8,128)S(1)} reshape(f32[16,16,128]{2,1,0:T(8,128)} %shard_map.64) | data formatting | bytes 262144 | tf_op jit(solution)/shard_map/reshape | solution.py:506
  64.1 0.8 %copy.8 = f32[16,25,64]{2,0,1:T(8,128)} copy(f32[16,25,64]{2,1,0:T(8,128)S(1)} %bitcast.5) | data formatting | bytes 204800

commit v7 on v6

--- a/solution.py
+++ b/solution.py
@@ -68,7 +68,7 @@
                 act(lax.rem(b + off(k, G // 2), G))
             return carry
 
-        lax.fori_loop(0, G - 1, one, 0, unroll=3)
+        lax.fori_loop(0, G - 1, one, 0)
 
     names = []
 

time: 65 us -> 65.1 us (level)
  no operation moved by 1% of the time
where the time goes in v7:
time: 65.1 us; the launch traced here: 65 us
  Pallas kernels  63.2 us (97%)
  local copies, waits for them, and re-layouts  1.81 us (3%)
    pallas_call x1, Pallas kernels, shards(): pl.pallas_call(body, out_shape=jax.ShapeDtypeStruct((G, G, PAIR), F32), i...  63.2 us

profile of v7, /device:TPU:1, one launch (start us, length us, event | category | flops | bytes accessed | tf_op | source)
XLA Modules:
  0.0 65.0 jit_solution(16264207986816298682)
XLA Ops:
  0.0 63.2 %shard_map.64 = f32[16,16,128]{2,1,0:T(8,128)} custom-call(bf16[25,16,64]{2,1,0:T(8,128)(2,1)} %bitcast.7, f32[25,2,25]{2,1,0:T(2,128)} %bitcast.9, bf16[2,2,32,128]{3,2,1,0:T(8,128)(2,1)} %bitcast.8, f32[2,16,64]{2,1,0:T(8,128)} %dec_hbm.1, f32[2,64]{1,0:T(2,128)} %skip_hbm.1, bf16[2,2,32,1024]{3,2,1,0:T(8,128)(2,1)} %bitcast.6), custom_call_target="tpu_custom_call" | custom-call | tf_op jit(solution)/shard_map/pallas_call | solution.py:451
  63.2 1.0 %reshape.11 = f32[16,32,64]{2,1,0:T(8,128)S(1)} reshape(f32[16,16,128]{2,1,0:T(8,128)} %shard_map.64) | data formatting | bytes 262144 | tf_op jit(solution)/shard_map/reshape | solution.py:506
  64.2 0.8 %copy.8 = f32[16,25,64]{2,0,1:T(8,128)} copy(f32[16,25,64]{2,1,0:T(8,128)S(1)} %bitcast.5) | data formatting | bytes 204800
